TPU v7x, 32 devices: a whole 2x2x4 slice. The times are simulated.
32 devices in a mesh: px: 2 (over y), py: 4 (over z), case: 4 (over x, core).
Axes of the slice: x: 2, y: 2, z: 4, core: 2. Of those that a mesh axis runs over, the one named last changes fastest.
Arguments:
- comp_type: int32 [1024], P(('px', 'py')), may hold values from 0 to 7
- stiffness: float32 [1024], P(('px', 'py')), may hold values from 0.3 to 3
- near_port: int32 [1024], P(('px', 'py')), may hold values from 0 to 127
- far_owner: int32 [1024, 1], P(('px', 'py')), may hold values from 0 to 7; in each aligned block of 128 rows (0 to 127, 128 to 255, ...) at most 24 rows name the same one
- far_port: int32 [1024], P(('px', 'py')), may hold values from 0 to 127
- bubble_load: float32 [64, 32, 1024], P(None, 'case', ('px', 'py')), may hold values from -6 to 6
- port_load: float32 [48, 32, 1024], P(None, 'case', ('px', 'py')), may hold values from -3 to 3
- bubble_inverse: float32 [8, 64, 64], replicated, may hold values from -1.5 to 2, as said below
- coupling: float32 [8, 96, 64], replicated, may hold values from -0.1 to 0.1
- port_block: float32 [8, 96, 96], replicated, may hold values from -3 to 8, as said below
Outputs:
- port_solution: float32 [48, 32, 1024], P(None, 'case', ('px', 'py'))
- port_residual: float32 [48, 32, 1024], P(None, 'case', ('px', 'py'))
- bubble_solution: float32 [64, 32, 1024], P(None, 'case', ('px', 'py'))
Inputs may be any that keep to these rules, and one draw needn't show every extreme that they name: `far_owner`: among the 128 components of one partition, at most 24 name the same owner, a bound that some block reaches. `bubble_inverse`: each matrix is symmetric positive definite. `port_block`: each matrix is symmetric positive definite.
All inputs are finite; a program needn't handle non-finite values.
Results may differ from a plain program's by a relative error of at most 0.00016.
Values sent between devices are 32-bit elements; how exact they have to be, the bound alone decides.
A program may use at most 64 MiB of HBM per device.

v0:
```python
import jax
import jax.numpy as jnp
from jax import lax
from jax.experimental import pallas as pl
from jax.experimental.pallas import tpu as pltpu
from jax.sharding import PartitionSpec as P

HIGH = lax.Precision.HIGHEST
F32 = jnp.float32
BF16 = jnp.bfloat16
MESH = pl.DeviceIdType.MESH
NT = (((1,), (1,)), ((), ()))
TN = (((0,), (0,)), ((), ()))


def split(x):
    top = x.astype(BF16)
    return top, (x - top.astype(F32)).astype(BF16)


def mm(a, b):
    return jnp.dot(a, b, preferred_element_type=F32)


def exact(a, b, dims=(((1,), (0,)), ((), ()))):
    return lax.dot_general(a, b, dims, precision=HIGH, preferred_element_type=F32)


def gauss_solve(matrix, target):
    n = matrix.shape[0]
    aug = jnp.concatenate([matrix, target], axis=1)
    rows = lax.broadcasted_iota(jnp.int32, aug.shape, 0)
    for j in range(n):
        row = aug[j:j + 1, :]
        row = row / row[:, j:j + 1]
        aug = jnp.where(rows == j, row, aug - aug[:, j:j + 1] * row)
    return aug[:, n:]


def kernel(
    sizes,
    idx_ref,
    stiff_ref,
    bload_ref,
    pload_ref,
    binv_ref,
    coup_ref,
    pblock_ref,
    sol_ref,
    res_ref,
    bub_ref,
    ask_send,
    ask_recv,
    far_send,
    far_recv,
    nat,
    gath,
    rows_all,
    gram_send,
    gram_recv,
    inv_keep,
    part_ssem,
    part_rsem,
    case_ssem,
    case_rsem,
):
    parts, npy, nq, depth = sizes
    kinds = binv_ref.shape[0]
    modes, ncase, ncomp = bload_ref.shape
    pd = pload_ref.shape[0]
    nport = pload_ref.shape[2]
    slots = parts * depth
    allcase = nq * ncase
    my_x, my_y, my_c = lax.axis_index("px"), lax.axis_index("py"), lax.axis_index("case")
    me = my_x * npy + my_y

    def part_id(step):
        other = lax.rem(me + step + parts, parts)
        return (other // npy, lax.rem(other, npy), my_c)

    def case_id(step):
        return (my_x, my_y, lax.rem(my_c + step, nq))

    barrier = pltpu.get_barrier_semaphore()

    def greet_part(i, _):
        pl.semaphore_signal(barrier, inc=1, device_id=part_id(i), device_id_type=MESH)
        return 0

    lax.fori_loop(1, parts, greet_part, 0)
    for i in range(1, nq):
        pl.semaphore_signal(barrier, inc=1, device_id=case_id(i), device_id_type=MESH)

    kind_row = idx_ref[0:1, :]
    near_row = idx_ref[1:2, :]
    owner_row = idx_ref[2:3, :]
    far_row = idx_ref[3:4, :]

    def as_column(row):
        return jnp.broadcast_to(row.astype(F32), (ncomp, ncomp)).T

    sub = lax.broadcasted_iota(jnp.int32, (ncomp, ncomp), 0)
    lane = lax.broadcasted_iota(jnp.int32, (ncomp, ncomp), 1)
    same = (as_column(owner_row) == owner_row.astype(F32)) & (sub < lane)
    rank = jnp.sum(jnp.where(same, 1.0, 0.0), axis=0, keepdims=True).astype(jnp.int32)
    slot_row = lax.rem(owner_row - me + parts, parts) * depth + rank
    slot_sub = lax.broadcasted_iota(jnp.int32, (slots, ncomp), 0)
    slot_f = jnp.where(slot_sub == slot_row, 1.0, 0.0)
    slot_pick = slot_f.astype(BF16)
    wanted = jnp.sum(slot_f * (far_row + 1).astype(F32), axis=1, keepdims=True) - 1.0
    wanted = jnp.broadcast_to(wanted, (slots, nport)).reshape(parts, depth, nport)
    ask_send[...] = wanted
    ask_recv[0] = wanted[0]
    near_in = jnp.where(sub == near_row, 1.0, 0.0).astype(BF16)
    near_out = jnp.where(lane.astype(F32) == as_column(near_row), 1.0, 0.0).astype(BF16)

    pl.semaphore_wait(barrier, parts - 1 + nq - 1)

    def send_parts(src, dst, e, sign):
        def body(i, _):
            pltpu.make_async_remote_copy(
                src_ref=src(i),
                dst_ref=dst(i),
                send_sem=part_ssem.at[e],
                recv_sem=part_rsem.at[e],
                device_id=part_id(i if sign > 0 else -i),
                device_id_type=MESH,
            ).start()
            return 0

        if parts <= 8:
            for i in range(1, parts):
                body(i, 0)
        else:
            lax.fori_loop(1, parts, body, 0)

    def wait_on(ref, sem):
        pltpu.make_async_copy(ref, ref, sem).wait()

    rest = pl.ds(1, parts - 1)
    send_parts(lambda i: ask_send.at[i], lambda i: ask_recv.at[i], 6, 1)

    red = [exact(coup_ref[t], binv_ref[t]) for t in range(kinds)]
    schur = [pblock_ref[t] - exact(red[t], coup_ref[t], NT) for t in range(kinds)]
    inv_tab = split(jnp.concatenate([binv_ref[t] for t in range(kinds)], axis=1))
    coup_tab = split(jnp.concatenate([coup_ref[t] for t in range(kinds)], axis=1))
    schur_tab = split(jnp.concatenate(schur, axis=1))
    red_tab = split(jnp.concatenate([r.T for r in red], axis=1))

    def tile_cases(row):
        return jnp.concatenate([row] * ncase, axis=1)

    stiff = tile_cases(stiff_ref[...])
    kind_all = tile_cases(kind_row)
    masks = [jnp.where(kind_all == t, 1.0, 0.0).astype(BF16) for t in range(kinds)]

    def apply_tables(tab, x):
        top, low = split(x)
        xt = jnp.concatenate([top * m for m in masks], axis=0)
        xl = jnp.concatenate([low * m for m in masks], axis=0)
        return mm(tab[0], xt) + mm(tab[0], xl) + mm(tab[1], xt)

    def wide(field, rows):
        return jnp.concatenate(
            [field[k * rows:(k + 1) * rows] for k in range(ncase)], axis=1
        )

    def tall(x):
        return jnp.concatenate(
            [x[:, k * ncomp:(k + 1) * ncomp] for k in range(ncase)], axis=0
        )

    def pick(x, onehot):
        top, low = split(x)
        return mm(jnp.concatenate([top, low], axis=1), jnp.concatenate([onehot, onehot], axis=0))

    def start_far(e, onehot, x, sign):
        top, low = split(x)
        out = lax.dot_general(
            jnp.concatenate([onehot, onehot], axis=1),
            jnp.concatenate([top, low], axis=1),
            NT,
            preferred_element_type=F32,
        ).reshape(parts, depth, x.shape[0])
        far_send[e] = out
        far_recv[e, 0] = out[0]
        send_parts(lambda i: far_send.at[e, i], lambda i: far_recv.at[e, i], e, sign)

    def finish_far(e, onehot):
        wait_on(far_recv.at[e, rest], part_rsem.at[e])
        got = far_recv[e].reshape(slots, ncase * pd).T
        top, low = split(got)
        return mm(top, onehot) + mm(low, onehot)

    def publish(f, field):
        for k in range(ncase):
            nat[f, :, k, :] = field[k * pd:(k + 1) * pd]
        for i in range(1, nq):
            pltpu.make_async_remote_copy(
                src_ref=nat.at[f],
                dst_ref=gath.at[f, i],
                send_sem=case_ssem.at[f],
                recv_sem=case_rsem.at[f],
                device_id=case_id(i),
                device_id_type=MESH,
            ).start()

    def collect(f):
        wait_on(gath.at[f, pl.ds(1, nq - 1)], case_rsem.at[f])

        def body(d, _):
            cols = pl.ds(pl.multiple_of(d * nport, nport), nport)
            rows_all[pl.ds(f * allcase, ncase), cols] = nat[f, d]
            for q in range(1, nq):
                rows_all[pl.ds(f * allcase + q * ncase, ncase), cols] = gath[f, q, d]
            return 0

        lax.fori_loop(0, pd, body, 0)

    def start_gram(s, value):
        h, w = value.shape
        gram_send[s] = jnp.zeros(gram_send.shape[1:], F32)
        gram_send[s, 0:h, 0:w] = value
        gram_recv[s, 0] = gram_send[s]
        send_parts(lambda i: gram_send.at[s], lambda i: gram_recv.at[s, i], 7 + s, 1)

    def finish_gram(s):
        wait_on(gram_recv.at[s, rest], part_rsem.at[7 + s])
        return jnp.sum(gram_recv[s], axis=0)

    def sym(g):
        return 0.5 * (g + g.T)

    loads = jnp.concatenate([bload_ref[:, k, :] for k in range(ncase)], axis=1)
    lifted = apply_tables(inv_tab, loads)
    inv_keep[...] = lifted
    condensed = -apply_tables(coup_tab, lifted)
    start_far(0, slot_pick, tall(condensed[pd:]), 1)
    own = jnp.concatenate([pload_ref[:, k, :] for k in range(ncase)], axis=0)
    own = own + pick(tall(condensed[:pd]), near_out)
    wait_on(ask_recv.at[rest], part_rsem.at[6])
    port_lane = lax.broadcasted_iota(jnp.int32, (slots, nport), 1).astype(F32)
    asked_pick = jnp.where(ask_recv[...].reshape(slots, nport) == port_lane, 1.0, 0.0).astype(BF16)
    base = own + finish_far(0, asked_pick)
    publish(0, base)

    def spread_start(e, field):
        start_far(e, asked_pick, field, -1)
        return pick(field, near_in)

    def spread_finish(e, near):
        far = finish_far(e, slot_pick)
        return jnp.concatenate([wide(near, pd), wide(far, pd)], axis=0)

    def operate_start(e, near):
        y = apply_tables(schur_tab, spread_finish(e, near)) * stiff
        start_far(e + 1, slot_pick, tall(y[pd:]), 1)
        return pick(tall(y[:pd]), near_out)

    near = spread_start(1, base)
    own = operate_start(1, near)
    first = own + finish_far(2, asked_pick)
    publish(1, first)
    near = spread_start(3, first)
    collect(0)
    own = operate_start(3, near)
    collect(1)
    pair = rows_all[0:2 * allcase, :]
    start_gram(0, exact(pair, pair, NT))
    second = own + finish_far(4, asked_pick)
    publish(2, second)

    n = allcase
    grams = finish_gram(0)
    g00 = sym(grams[0:n, 0:n])
    g01 = sym(grams[0:n, n:2 * n])
    g11 = sym(grams[n:2 * n, n:2 * n])
    step1 = gauss_solve(g01, g00)
    cross = exact(g01, step1)
    g1 = sym(g00 - cross - cross.T + exact(step1, exact(g11, step1), TN))
    turn = gauss_solve(g00, g1)
    eye = jnp.where(
        lax.broadcasted_iota(jnp.int32, (n, n), 0) == lax.broadcasted_iota(jnp.int32, (n, n), 1),
        1.0,
        0.0,
    )
    lead = turn + eye
    mixed = exact(lead, exact(g11, step1), TN)
    known = exact(lead, exact(g01, lead), TN) - mixed - mixed.T

    collect(2)
    start_gram(1, exact(rows_all[n:2 * n, :], rows_all[2 * n:3 * n, :], NT))
    g12 = sym(finish_gram(1)[0:n, 0:n])
    curve = sym(known + exact(step1, exact(g12, step1), TN))
    step2 = gauss_solve(curve, g1)
    alpha = step1 + exact(lead, step2)
    beta = exact(step1, step2)
    at = alpha.T[0:ncase]
    bt = beta.T[0:ncase]
    zero = jnp.zeros_like(at)
    coefs = jnp.concatenate(
        [
            jnp.concatenate([at, -bt, zero], axis=1),
            jnp.concatenate([zero, -at, bt], axis=1),
        ],
        axis=0,
    )
    ctop, clow = split(coefs)
    both = jnp.concatenate([ctop, clow], axis=0)
    vtop, vlow = split(rows_all[...])
    part_a = mm(both, vtop)
    mixed_rows = part_a[0:2 * ncase] + part_a[2 * ncase:] + mm(ctop, vlow)
    for d in range(pd):
        cols = slice(d * nport, (d + 1) * nport)
        sol_ref[d] = mixed_rows[0:ncase, cols]
        res_ref[d] = nat[0, d] + mixed_rows[ncase:, cols]

    answer = jnp.concatenate([sol_ref[:, k, :] for k in range(ncase)], axis=0)
    near = spread_start(5, answer)
    scaled = inv_keep[...] / stiff
    back = scaled - apply_tables(red_tab, spread_finish(5, near))
    for k in range(ncase):
        bub_ref[:, k, :] = back[:, k * ncomp:(k + 1) * ncomp]

    wait_on(ask_send.at[rest], part_ssem.at[6])
    for e in range(6):
        wait_on(far_send.at[e, rest], part_ssem.at[e])
    for s in range(2):
        wait_on(gram_recv.at[s, rest], part_ssem.at[7 + s])
    for f in range(3):
        wait_on(gath.at[f, pl.ds(1, nq - 1)], case_ssem.at[f])


def local(
    comp_type,
    stiffness,
    near_port,
    far_owner,
    far_port,
    bubble_load,
    port_load,
    bubble_inverse,
    coupling,
    port_block,
):
    npy = lax.axis_size("py")
    parts = lax.axis_size("px") * npy
    nq = lax.axis_size("case")
    ncomp = comp_type.shape[0]
    modes, ncase, _ = bubble_load.shape
    pd, _, nport = port_load.shape
    cap = 3 * ncomp // (2 * parts)
    depth = -(-cap // 8) * 8
    allcase = nq * ncase
    idx = jnp.stack([comp_type, near_port, far_owner[:, 0], far_port])
    vmem = pl.BlockSpec(memory_space=pltpu.VMEM)

    def body(*refs):
        kernel((parts, npy, nq, depth), *refs)

    return pl.pallas_call(
        body,
        out_shape=(
            jax.ShapeDtypeStruct(port_load.shape, F32),
            jax.ShapeDtypeStruct(port_load.shape, F32),
            jax.ShapeDtypeStruct(bubble_load.shape, F32),
        ),
        in_specs=[vmem] * 7,
        out_specs=(vmem, vmem, vmem),
        scratch_shapes=[
            pltpu.VMEM((parts, depth, nport), F32),
            pltpu.VMEM((parts, depth, nport), F32),
            pltpu.VMEM((6, parts, depth, ncase * pd), F32),
            pltpu.VMEM((6, parts, depth, ncase * pd), F32),
            pltpu.VMEM((3, pd, ncase, nport), F32),
            pltpu.VMEM((3, nq, pd, ncase, nport), F32),
            pltpu.VMEM((3 * allcase, pd * nport), F32),
            pltpu.VMEM((2, 2 * allcase, 128), F32),
            pltpu.VMEM((2, parts, 2 * allcase, 128), F32),
            pltpu.VMEM((modes, ncase * ncomp), F32),
            pltpu.SemaphoreType.DMA((9,)),
            pltpu.SemaphoreType.DMA((9,)),
            pltpu.SemaphoreType.DMA((3,)),
            pltpu.SemaphoreType.DMA((3,)),
        ],
        compiler_params=pltpu.CompilerParams(
            collective_id=0, has_side_effects=True, vmem_limit_bytes=60 * 1024 * 1024
        ),
        name="condensed_solve",
    )(
        idx,
        stiffness.reshape(1, ncomp),
        bubble_load,
        port_load,
        bubble_inverse,
        coupling,
        port_block,
    )


def solution(mesh):
    placed = (
        P(("px", "py")),
        P(("px", "py")),
        P(("px", "py")),
        P(("px", "py"), None),
        P(("px", "py")),
        P(None, "case", ("px", "py")),
        P(None, "case", ("px", "py")),
        P(),
        P(),
        P(),
    )
    return jax.shard_map(
        local,
        mesh=mesh,
        in_specs=placed,
        out_specs=(
            P(None, "case", ("px", "py")),
            P(None, "case", ("px", "py")),
            P(None, "case", ("px", "py")),
        ),
        check_vma=False,
    )
```

profile of v0, /device:TPU:0, one launch (start us, length us, event | category | flops | bytes accessed | tf_op | source)
XLA Modules:
  0.0 97.8 jit_solution(8604335922201866525)
XLA Ops:
  0.6 0.0 copy-start.5
  0.6 0.0 copy-start.2
  0.7 0.0 copy-start.3
  0.7 0.0 copy-start.4
  0.7 0.6 copy-done.5
  1.3 0.0 copy-done.2
  1.3 0.0 copy-done.3
  1.3 0.0 copy-done.4
  1.3 0.6 pad_add_fusion.refs_0_
  1.9 1.9 %copy.13.refs_5_ = f32[8,96,64]{2,1,0:T(8,128)} copy(f32[8,96,64]{1,2,0:T(8,128)} %param.18) | data formatting | bytes 393216 | tf_op args[8]
  3.8 90.6 %condensed_solve.1 = (f32[48,8,128]{2,1,0:T(8,128)}, f32[48,8,128]{2,1,0:T(8,128)}, f32[64,8,128]{2,1,0:T(8,128)}) custom-call(s32[4,128]{1,0:T(4,128)} %pad_add_fusion.refs_0_, f32[1,128]{1,0:T(1,128)} %bitcast.5, f32[64,8,128]{2,1,0:T(8,128)} %refs_2_.1, f32[48,8,128]{2,1,0:T(8,128)} %refs_3_.1, f32[8,64,64]{2,1,0:T(8,128)} %refs_4_.1, ...), custom_call_target="tpu_custom_call" | custom-call | tf_op jit(solution)/shard_map/condensed_solve/pallas_call | solution.py:361
  94.4 0.0 copy-start.1
  94.5 1.7 %copy.17 = f32[48,8,128]{2,1,0:T(8,128)} copy(f32[48,8,128]{2,1,0:T(8,128)} %get-tuple-element.6) | data formatting | bytes 393216
  96.1 0.0 copy-done.1
  96.1 0.0 copy-start
  96.1 0.7 copy.18
  96.8 0.3 copy-done
  97.1 0.7 copy.19
Async XLA Ops:
  0.6 0.7 copy-start.5
  0.6 0.7 copy-start.2
  0.7 0.7 copy-start.3
  0.7 0.7 copy-start.4
  94.4 1.7 %copy-start.1 = (f32[48,8,128]{2,1,0:T(8,128)S(1)}, f32[48,8,128]{2,1,0:T(8,128)}, u32[]{:S(2)}) copy-start(f32[48,8,128]{2,1,0:T(8,128)} %get-tuple-element.7) | copy-start | bytes 589828
  96.1 1.0 %copy-start = (f32[64,8,128]{2,1,0:T(8,128)S(1)}, f32[64,8,128]{2,1,0:T(8,128)}, u32[]{:S(2)}) copy-start(f32[64,8,128]{2,1,0:T(8,128)} %get-tuple-element.8) | copy-start | bytes 786436
where the time goes:
time: 98.1 us; the launch traced here: 97.8 us
  Pallas kernels  90.6 us (92%)
  local copies, waits for them, and re-layouts  5.93 us (6%)
    pallas_call x1, Pallas kernels, local(): pl.pallas_call(body, out_shape=(jax.ShapeDtypeStruct(port_load.shape, F32...  90.6 us
    unnamed x16, local copies, waits for them, and re-layouts  5.93 us

commit v1 on v0

--- a/solution.py
+++ b/solution.py
@@ -56,14 +56,18 @@
     nat,
     gath,
     rows_all,
-    gram_send,
-    gram_recv,
+    pair_send,
+    pair_recv,
+    last_send,
+    last_recv,
     inv_keep,
+    nat_far,
     part_ssem,
     part_rsem,
     case_ssem,
     case_rsem,
 ):
+    gram_refs = ((pair_send, pair_recv), (last_send, last_recv))
     parts, npy, nq, depth = sizes
     kinds = binv_ref.shape[0]
     modes, ncase, ncomp = bload_ref.shape
@@ -140,12 +144,12 @@
     rest = pl.ds(1, parts - 1)
     send_parts(lambda i: ask_send.at[i], lambda i: ask_recv.at[i], 6, 1)
 
-    red = [exact(coup_ref[t], binv_ref[t]) for t in range(kinds)]
-    schur = [pblock_ref[t] - exact(red[t], coup_ref[t], NT) for t in range(kinds)]
+    red_t = [exact(binv_ref[t], coup_ref[t], TN) for t in range(kinds)]
+    schur = [pblock_ref[t] - exact(red_t[t], coup_ref[t], TN) for t in range(kinds)]
     inv_tab = split(jnp.concatenate([binv_ref[t] for t in range(kinds)], axis=1))
-    coup_tab = split(jnp.concatenate([coup_ref[t] for t in range(kinds)], axis=1))
+    coup_tab = split(jnp.concatenate([coup_ref[t].T for t in range(kinds)], axis=1))
     schur_tab = split(jnp.concatenate(schur, axis=1))
-    red_tab = split(jnp.concatenate([r.T for r in red], axis=1))
+    red_tab = split(jnp.concatenate(red_t, axis=1))
 
     def tile_cases(row):
         return jnp.concatenate([row] * ncase, axis=1)
@@ -218,15 +222,22 @@
         lax.fori_loop(0, pd, body, 0)
 
     def start_gram(s, value):
-        h, w = value.shape
-        gram_send[s] = jnp.zeros(gram_send.shape[1:], F32)
-        gram_send[s, 0:h, 0:w] = value
-        gram_recv[s, 0] = gram_send[s]
-        send_parts(lambda i: gram_send.at[s], lambda i: gram_recv.at[s, i], 7 + s, 1)
+        sent, got = gram_refs[s]
+        folded = jnp.concatenate(
+            [value[8 * r:8 * r + 8] for r in range(value.shape[0] // 8)], axis=1
+        )
+        sent[...] = folded
+        got[0] = folded
+        send_parts(lambda i: sent, lambda i: got.at[i], 7 + s, 1)
 
     def finish_gram(s):
-        wait_on(gram_recv.at[s, rest], part_rsem.at[7 + s])
-        return jnp.sum(gram_recv[s], axis=0)
+        got = gram_refs[s][1]
+        wait_on(got.at[rest], part_rsem.at[7 + s])
+        total = jnp.sum(got[...], axis=0)
+        return jnp.concatenate(
+            [total[:, allcase * r:allcase * (r + 1)] for r in range(total.shape[1] // allcase)],
+            axis=0,
+        )
 
     def sym(g):
         return 0.5 * (g + g.T)
@@ -250,6 +261,7 @@
 
     def spread_finish(e, near):
         far = finish_far(e, slot_pick)
+        publish(3 + e // 2, far)
         return jnp.concatenate([wide(near, pd), wide(far, pd)], axis=0)
 
     def operate_start(e, near):
@@ -266,15 +278,16 @@
     own = operate_start(3, near)
     collect(1)
     pair = rows_all[0:2 * allcase, :]
-    start_gram(0, exact(pair, pair, NT))
+    square = exact(pair, pair, NT)
+    start_gram(0, jnp.concatenate([square[0:allcase, 0:allcase], square[0:allcase, allcase:], square[allcase:, allcase:]], axis=0))
     second = own + finish_far(4, asked_pick)
     publish(2, second)
 
     n = allcase
     grams = finish_gram(0)
-    g00 = sym(grams[0:n, 0:n])
-    g01 = sym(grams[0:n, n:2 * n])
-    g11 = sym(grams[n:2 * n, n:2 * n])
+    g00 = sym(grams[0:n])
+    g01 = sym(grams[n:2 * n])
+    g11 = sym(grams[2 * n:3 * n])
     step1 = gauss_solve(g01, g00)
     cross = exact(g01, step1)
     g1 = sym(g00 - cross - cross.T + exact(step1, exact(g11, step1), TN))
@@ -290,7 +303,7 @@
 
     collect(2)
     start_gram(1, exact(rows_all[n:2 * n, :], rows_all[2 * n:3 * n, :], NT))
-    g12 = sym(finish_gram(1)[0:n, 0:n])
+    g12 = sym(finish_gram(1))
     curve = sym(known + exact(step1, exact(g12, step1), TN))
     step2 = gauss_solve(curve, g1)
     alpha = step1 + exact(lead, step2)
@@ -307,7 +320,7 @@
     )
     ctop, clow = split(coefs)
     both = jnp.concatenate([ctop, clow], axis=0)
-    vtop, vlow = split(rows_all[...])
+    vtop, vlow = split(rows_all[0:3 * allcase, :])
     part_a = mm(both, vtop)
     mixed_rows = part_a[0:2 * ncase] + part_a[2 * ncase:] + mm(ctop, vlow)
     for d in range(pd):
@@ -316,18 +329,29 @@
         res_ref[d] = nat[0, d] + mixed_rows[ncase:, cols]
 
     answer = jnp.concatenate([sol_ref[:, k, :] for k in range(ncase)], axis=0)
-    near = spread_start(5, answer)
+    collect(3)
+    collect(4)
+    ftop, flow = split(rows_all[3 * allcase:, :])
+    lead_a = jnp.concatenate([ctop[0:ncase, 0:2 * n], clow[0:ncase, 0:2 * n]], axis=0)
+    part_f = mm(lead_a, ftop)
+    far_rows = part_f[0:ncase] + part_f[ncase:] + mm(ctop[0:ncase, 0:2 * n], flow)
+    for d in range(pd):
+        nat_far[d] = far_rows[:, d * nport:(d + 1) * nport]
+    near = wide(pick(answer, near_in), pd)
+    ends = jnp.concatenate(
+        [near, jnp.concatenate([nat_far[:, k, :] for k in range(ncase)], axis=1)], axis=0
+    )
     scaled = inv_keep[...] / stiff
-    back = scaled - apply_tables(red_tab, spread_finish(5, near))
+    back = scaled - apply_tables(red_tab, ends)
     for k in range(ncase):
         bub_ref[:, k, :] = back[:, k * ncomp:(k + 1) * ncomp]
 
     wait_on(ask_send.at[rest], part_ssem.at[6])
-    for e in range(6):
+    for e in range(5):
         wait_on(far_send.at[e, rest], part_ssem.at[e])
     for s in range(2):
-        wait_on(gram_recv.at[s, rest], part_ssem.at[7 + s])
-    for f in range(3):
+        wait_on(gram_refs[s][1].at[rest], part_ssem.at[7 + s])
+    for f in range(5):
         wait_on(gath.at[f, pl.ds(1, nq - 1)], case_ssem.at[f])
 
 
@@ -370,18 +394,21 @@
         scratch_shapes=[
             pltpu.VMEM((parts, depth, nport), F32),
             pltpu.VMEM((parts, depth, nport), F32),
-            pltpu.VMEM((6, parts, depth, ncase * pd), F32),
-            pltpu.VMEM((6, parts, depth, ncase * pd), F32),
-            pltpu.VMEM((3, pd, ncase, nport), F32),
-            pltpu.VMEM((3, nq, pd, ncase, nport), F32),
-            pltpu.VMEM((3 * allcase, pd * nport), F32),
-            pltpu.VMEM((2, 2 * allcase, 128), F32),
-            pltpu.VMEM((2, parts, 2 * allcase, 128), F32),
+            pltpu.VMEM((5, parts, depth, ncase * pd), F32),
+            pltpu.VMEM((5, parts, depth, ncase * pd), F32),
+            pltpu.VMEM((5, pd, ncase, nport), F32),
+            pltpu.VMEM((5, nq, pd, ncase, nport), F32),
+            pltpu.VMEM((5 * allcase, pd * nport), F32),
+            pltpu.VMEM((8, 3 * allcase * allcase // 8), F32),
+            pltpu.VMEM((parts, 8, 3 * allcase * allcase // 8), F32),
+            pltpu.VMEM((8, allcase * allcase // 8), F32),
+            pltpu.VMEM((parts, 8, allcase * allcase // 8), F32),
             pltpu.VMEM((modes, ncase * ncomp), F32),
+            pltpu.VMEM((pd, ncase, nport), F32),
             pltpu.SemaphoreType.DMA((9,)),
             pltpu.SemaphoreType.DMA((9,)),
-            pltpu.SemaphoreType.DMA((3,)),
-            pltpu.SemaphoreType.DMA((3,)),
+            pltpu.SemaphoreType.DMA((5,)),
+            pltpu.SemaphoreType.DMA((5,)),
         ],
         compiler_params=pltpu.CompilerParams(
             collective_id=0, has_side_effects=True, vmem_limit_bytes=60 * 1024 * 1024
@@ -393,7 +420,7 @@
         bubble_load,
         port_load,
         bubble_inverse,
-        coupling,
+        jnp.swapaxes(coupling, 1, 2),
         port_block,
     )
 

time: 98.1 us -> 80.3 us (0.82)
  Pallas kernels: 90.6 us -> 74.1 us
  local copies, waits for them, and re-layouts: 5.93 us -> 4.05 us
    pallas_call x1, Pallas kernels: 90.6 us -> 74.1 us  [local(): pl.pallas_call(body, out_shape=(jax.ShapeDtypeStruct(port_load.shape, F32...]
    unnamed x16 -> x15, local copies, waits for them, and re-layouts: 5.93 us -> 4.05 us
where the time goes in v1:
time: 80.3 us; the launch traced here: 79.4 us
  Pallas kernels  74.1 us (92%)
  local copies, waits for them, and re-layouts  4.05 us (5%)
    pallas_call x1, Pallas kernels, local(): pl.pallas_call(body, out_shape=(jax.ShapeDtypeStruct(port_load.shape, F32...  74.1 us
    unnamed x15, local copies, waits for them, and re-layouts  4.05 us

profile of v1, /device:TPU:0, one launch (start us, length us, event | category | flops | bytes accessed | tf_op | source)
XLA Modules:
  0.0 79.4 jit_solution(10941366037453482381)
XLA Ops:
  0.6 0.0 copy-start.5
  0.6 0.0 copy-start.2
  0.7 0.0 copy-start.3
  0.7 0.0 copy-start.4
  0.7 0.6 copy-done.5
  1.3 0.0 copy-done.2
  1.3 0.0 copy-done.3
  1.3 0.0 copy-done.4
  1.3 0.6 pad_add_fusion.refs_0_
  1.9 74.1 %condensed_solve.1 = (f32[48,8,128]{2,1,0:T(8,128)}, f32[48,8,128]{2,1,0:T(8,128)}, f32[64,8,128]{2,1,0:T(8,128)}) custom-call(s32[4,128]{1,0:T(4,128)} %pad_add_fusion.refs_0_, f32[1,128]{1,0:T(1,128)} %bitcast.7, f32[64,8,128]{2,1,0:T(8,128)} %refs_2_.1, f32[48,8,128]{2,1,0:T(8,128)} %refs_3_.1, f32[8,64,64]{2,1,0:T(8,128)} %refs_4_.1, ...), custom_call_target="tpu_custom_call" | custom-call | tf_op jit(solution)/shard_map/condensed_solve/pallas_call | solution.py:385
  76.0 0.0 copy-start.1
  76.0 1.7 %copy.16 = f32[48,8,128]{2,1,0:T(8,128)} copy(f32[48,8,128]{2,1,0:T(8,128)} %get-tuple-element.6) | data formatting | bytes 393216
  77.7 0.0 copy-done.1
  77.7 0.0 copy-start
  77.7 0.7 copy.17
  78.4 0.3 copy-done
  78.7 0.7 copy.18
Async XLA Ops:
  0.6 0.7 copy-start.5
  0.6 0.7 copy-start.2
  0.7 0.7 copy-start.3
  0.7 0.7 copy-start.4
  76.0 1.7 %copy-start.1 = (f32[48,8,128]{2,1,0:T(8,128)S(1)}, f32[48,8,128]{2,1,0:T(8,128)}, u32[]{:S(2)}) copy-start(f32[48,8,128]{2,1,0:T(8,128)} %get-tuple-element.7) | copy-start | bytes 589828
  77.7 1.0 %copy-start = (f32[64,8,128]{2,1,0:T(8,128)S(1)}, f32[64,8,128]{2,1,0:T(8,128)}, u32[]{:S(2)}) copy-start(f32[64,8,128]{2,1,0:T(8,128)} %get-tuple-element.8) | copy-start | bytes 786436

commit v2 on v1

--- a/solution.py
+++ b/solution.py
@@ -68,7 +68,7 @@
     case_rsem,
 ):
     gram_refs = ((pair_send, pair_recv), (last_send, last_recv))
-    parts, npy, nq, depth = sizes
+    parts, npy, nq, depth, width, chunks = sizes
     kinds = binv_ref.shape[0]
     modes, ncase, ncomp = bload_ref.shape
     pd = pload_ref.shape[0]
@@ -83,7 +83,14 @@
         return (other // npy, lax.rem(other, npy), my_c)
 
     def case_id(step):
-        return (my_x, my_y, lax.rem(my_c + step, nq))
+        if nq == 4:
+            other = my_c + (step % 2) * (1 - 2 * lax.rem(my_c, 2))
+            other = other + (step // 2) * (2 - 4 * (my_c // 2))
+        else:
+            other = lax.rem(my_c + step, nq)
+        return (my_x, my_y, other)
+
+    direct = (1, 2) if nq == 4 else tuple(range(1, nq))
 
     barrier = pltpu.get_barrier_semaphore()
 
@@ -142,7 +149,7 @@
         pltpu.make_async_copy(ref, ref, sem).wait()
 
     rest = pl.ds(1, parts - 1)
-    send_parts(lambda i: ask_send.at[i], lambda i: ask_recv.at[i], 6, 1)
+    send_parts(lambda i: ask_send.at[i], lambda i: ask_recv.at[i], 0, 1)
 
     red_t = [exact(binv_ref[t], coup_ref[t], TN) for t in range(kinds)]
     schur = [pblock_ref[t] - exact(red_t[t], coup_ref[t], TN) for t in range(kinds)]
@@ -160,57 +167,70 @@
 
     def apply_tables(tab, x):
         top, low = split(x)
-        xt = jnp.concatenate([top * m for m in masks], axis=0)
-        xl = jnp.concatenate([low * m for m in masks], axis=0)
+        lanes = x.shape[1]
+        xt = jnp.concatenate([top * m[:, :lanes] for m in masks], axis=0)
+        xl = jnp.concatenate([low * m[:, :lanes] for m in masks], axis=0)
         return mm(tab[0], xt) + mm(tab[0], xl) + mm(tab[1], xt)
 
     def wide(field, rows):
         return jnp.concatenate(
-            [field[k * rows:(k + 1) * rows] for k in range(ncase)], axis=1
+            [field[k * rows:(k + 1) * rows] for k in range(field.shape[0] // rows)], axis=1
         )
 
     def tall(x):
         return jnp.concatenate(
-            [x[:, k * ncomp:(k + 1) * ncomp] for k in range(ncase)], axis=0
+            [x[:, k * ncomp:(k + 1) * ncomp] for k in range(x.shape[1] // ncomp)], axis=0
         )
 
     def pick(x, onehot):
         top, low = split(x)
         return mm(jnp.concatenate([top, low], axis=1), jnp.concatenate([onehot, onehot], axis=0))
 
-    def start_far(e, onehot, x, sign):
+    def start_far(e, j, onehot, x, sign):
         top, low = split(x)
         out = lax.dot_general(
             jnp.concatenate([onehot, onehot], axis=1),
             jnp.concatenate([top, low], axis=1),
             NT,
             preferred_element_type=F32,
-        ).reshape(parts, depth, x.shape[0])
-        far_send[e] = out
-        far_recv[e, 0] = out[0]
-        send_parts(lambda i: far_send.at[e, i], lambda i: far_recv.at[e, i], e, sign)
-
-    def finish_far(e, onehot):
-        wait_on(far_recv.at[e, rest], part_rsem.at[e])
-        got = far_recv[e].reshape(slots, ncase * pd).T
+        ).reshape(parts, depth, width)
+        far_send[e, j] = out
+        far_recv[e, j, 0] = out[0]
+        send_parts(
+            lambda i: far_send.at[e, j, i], lambda i: far_recv.at[e, j, i], 3 + e * chunks + j, sign
+        )
+
+    def finish_far(e, j, onehot):
+        wait_on(far_recv.at[e, j, rest], part_rsem.at[3 + e * chunks + j])
+        got = far_recv[e, j].reshape(slots, width).T
         top, low = split(got)
         return mm(top, onehot) + mm(low, onehot)
+
+    def send_case(f, src, block, step):
+        pltpu.make_async_remote_copy(
+            src_ref=src,
+            dst_ref=gath.at[f, block],
+            send_sem=case_ssem.at[f, block],
+            recv_sem=case_rsem.at[f, block],
+            device_id=case_id(step),
+            device_id_type=MESH,
+        ).start()
 
     def publish(f, field):
         for k in range(ncase):
             nat[f, :, k, :] = field[k * pd:(k + 1) * pd]
+        for i in reversed(direct):
+            send_case(f, nat.at[f], i, i)
+
+    def forward(f):
+        if nq == 4:
+            wait_on(gath.at[f, 2], case_rsem.at[f, 2])
+            send_case(f, gath.at[f, 2], 3, 1)
+
+    def collect(f):
         for i in range(1, nq):
-            pltpu.make_async_remote_copy(
-                src_ref=nat.at[f],
-                dst_ref=gath.at[f, i],
-                send_sem=case_ssem.at[f],
-                recv_sem=case_rsem.at[f],
-                device_id=case_id(i),
-                device_id_type=MESH,
-            ).start()
-
-    def collect(f):
-        wait_on(gath.at[f, pl.ds(1, nq - 1)], case_rsem.at[f])
+            if nq != 4 or i != 2:
+                wait_on(gath.at[f, i], case_rsem.at[f, i])
 
         def body(d, _):
             cols = pl.ds(pl.multiple_of(d * nport, nport), nport)
@@ -219,7 +239,7 @@
                 rows_all[pl.ds(f * allcase + q * ncase, ncase), cols] = gath[f, q, d]
             return 0
 
-        lax.fori_loop(0, pd, body, 0)
+        lax.fori_loop(0, pd, body, 0, unroll=4)
 
     def start_gram(s, value):
         sent, got = gram_refs[s]
@@ -228,11 +248,11 @@
         )
         sent[...] = folded
         got[0] = folded
-        send_parts(lambda i: sent, lambda i: got.at[i], 7 + s, 1)
+        send_parts(lambda i: sent, lambda i: got.at[i], 1 + s, 1)
 
     def finish_gram(s):
         got = gram_refs[s][1]
-        wait_on(got.at[rest], part_rsem.at[7 + s])
+        wait_on(got.at[rest], part_rsem.at[1 + s])
         total = jnp.sum(got[...], axis=0)
         return jnp.concatenate(
             [total[:, allcase * r:allcase * (r + 1)] for r in range(total.shape[1] // allcase)],
@@ -242,46 +262,72 @@
     def sym(g):
         return 0.5 * (g + g.T)
 
+    def part(x, j):
+        return x[j * width:(j + 1) * width]
+
     loads = jnp.concatenate([bload_ref[:, k, :] for k in range(ncase)], axis=1)
     lifted = apply_tables(inv_tab, loads)
     inv_keep[...] = lifted
     condensed = -apply_tables(coup_tab, lifted)
-    start_far(0, slot_pick, tall(condensed[pd:]), 1)
+    leaving = tall(condensed[pd:])
+    for j in range(chunks):
+        start_far(0, j, slot_pick, part(leaving, j), 1)
     own = jnp.concatenate([pload_ref[:, k, :] for k in range(ncase)], axis=0)
     own = own + pick(tall(condensed[:pd]), near_out)
-    wait_on(ask_recv.at[rest], part_rsem.at[6])
+    wait_on(ask_recv.at[rest], part_rsem.at[0])
     port_lane = lax.broadcasted_iota(jnp.int32, (slots, nport), 1).astype(F32)
     asked_pick = jnp.where(ask_recv[...].reshape(slots, nport) == port_lane, 1.0, 0.0).astype(BF16)
-    base = own + finish_far(0, asked_pick)
+
+    def arrive(e, own, onward):
+        pieces = []
+        for j in range(chunks):
+            piece = part(own, j) + finish_far(e, j, asked_pick)
+            if onward:
+                start_far(e + 1, j, asked_pick, piece, -1)
+            pieces.append(piece)
+        return jnp.concatenate(pieces, axis=0)
+
+    def operate(e, near):
+        cuts = [0, ((chunks - 1) * width) // pd, ncase] if chunks > 1 else [0, ncase]
+        far, near_y, far_y, sent, have = None, None, None, 0, 0
+        for a, b in zip(cuts[:-1], cuts[1:]):
+            while have * width < b * pd:
+                piece = finish_far(e, have, slot_pick)
+                far = piece if far is None else jnp.concatenate([far, piece], axis=0)
+                have += 1
+            rows = slice(a * pd, b * pd)
+            ends = jnp.concatenate([wide(near[rows], pd), wide(far[rows], pd)], axis=0)
+            y = apply_tables(schur_tab, ends) * stiff[:, a * ncomp:b * ncomp]
+            out = tall(y[pd:])
+            far_y = out if far_y is None else jnp.concatenate([far_y, out], axis=0)
+            out = tall(y[:pd])
+            near_y = out if near_y is None else jnp.concatenate([near_y, out], axis=0)
+            while (sent + 1) * width <= b * pd:
+                start_far(e + 1, sent, slot_pick, part(far_y, sent), 1)
+                sent += 1
+        return far, pick(near_y, near_out)
+
+    base = arrive(0, own, True)
     publish(0, base)
-
-    def spread_start(e, field):
-        start_far(e, asked_pick, field, -1)
-        return pick(field, near_in)
-
-    def spread_finish(e, near):
-        far = finish_far(e, slot_pick)
-        publish(3 + e // 2, far)
-        return jnp.concatenate([wide(near, pd), wide(far, pd)], axis=0)
-
-    def operate_start(e, near):
-        y = apply_tables(schur_tab, spread_finish(e, near)) * stiff
-        start_far(e + 1, slot_pick, tall(y[pd:]), 1)
-        return pick(tall(y[:pd]), near_out)
-
-    near = spread_start(1, base)
-    own = operate_start(1, near)
-    first = own + finish_far(2, asked_pick)
+    far_base, own = operate(1, pick(base, near_in))
+    publish(3, far_base)
+    forward(0)
+    first = arrive(2, own, True)
     publish(1, first)
-    near = spread_start(3, first)
+    near = pick(first, near_in)
+    forward(3)
     collect(0)
-    own = operate_start(3, near)
+    far_first, own = operate(3, near)
+    forward(1)
+    publish(4, far_first)
     collect(1)
     pair = rows_all[0:2 * allcase, :]
     square = exact(pair, pair, NT)
     start_gram(0, jnp.concatenate([square[0:allcase, 0:allcase], square[0:allcase, allcase:], square[allcase:, allcase:]], axis=0))
-    second = own + finish_far(4, asked_pick)
+    second = arrive(4, own, False)
     publish(2, second)
+    forward(4)
+    collect(3)
 
     n = allcase
     grams = finish_gram(0)
@@ -289,6 +335,7 @@
     g01 = sym(grams[n:2 * n])
     g11 = sym(grams[2 * n:3 * n])
     step1 = gauss_solve(g01, g00)
+    forward(2)
     cross = exact(g01, step1)
     g1 = sym(g00 - cross - cross.T + exact(step1, exact(g11, step1), TN))
     turn = gauss_solve(g00, g1)
@@ -301,6 +348,7 @@
     mixed = exact(lead, exact(g11, step1), TN)
     known = exact(lead, exact(g01, lead), TN) - mixed - mixed.T
 
+    collect(4)
     collect(2)
     start_gram(1, exact(rows_all[n:2 * n, :], rows_all[2 * n:3 * n, :], NT))
     g12 = sym(finish_gram(1))
@@ -329,8 +377,6 @@
         res_ref[d] = nat[0, d] + mixed_rows[ncase:, cols]
 
     answer = jnp.concatenate([sol_ref[:, k, :] for k in range(ncase)], axis=0)
-    collect(3)
-    collect(4)
     ftop, flow = split(rows_all[3 * allcase:, :])
     lead_a = jnp.concatenate([ctop[0:ncase, 0:2 * n], clow[0:ncase, 0:2 * n]], axis=0)
     part_f = mm(lead_a, ftop)
@@ -346,13 +392,15 @@
     for k in range(ncase):
         bub_ref[:, k, :] = back[:, k * ncomp:(k + 1) * ncomp]
 
-    wait_on(ask_send.at[rest], part_ssem.at[6])
+    wait_on(ask_send.at[rest], part_ssem.at[0])
     for e in range(5):
-        wait_on(far_send.at[e, rest], part_ssem.at[e])
+        for j in range(chunks):
+            wait_on(far_send.at[e, j, rest], part_ssem.at[3 + e * chunks + j])
     for s in range(2):
-        wait_on(gram_refs[s][1].at[rest], part_ssem.at[7 + s])
+        wait_on(gram_refs[s][1].at[rest], part_ssem.at[1 + s])
     for f in range(5):
-        wait_on(gath.at[f, pl.ds(1, nq - 1)], case_ssem.at[f])
+        for i in range(1, nq):
+            wait_on(nat.at[f], case_ssem.at[f, i])
 
 
 def local(
@@ -376,11 +424,13 @@
     cap = 3 * ncomp // (2 * parts)
     depth = -(-cap // 8) * 8
     allcase = nq * ncase
+    width = 128 if (ncase * pd) % 128 == 0 else ncase * pd
+    chunks = ncase * pd // width
     idx = jnp.stack([comp_type, near_port, far_owner[:, 0], far_port])
     vmem = pl.BlockSpec(memory_space=pltpu.VMEM)
 
     def body(*refs):
-        kernel((parts, npy, nq, depth), *refs)
+        kernel((parts, npy, nq, depth, width, chunks), *refs)
 
     return pl.pallas_call(
         body,
@@ -394,8 +444,8 @@
         scratch_shapes=[
             pltpu.VMEM((parts, depth, nport), F32),
             pltpu.VMEM((parts, depth, nport), F32),
-            pltpu.VMEM((5, parts, depth, ncase * pd), F32),
-            pltpu.VMEM((5, parts, depth, ncase * pd), F32),
+            pltpu.VMEM((5, chunks, parts, depth, width), F32),
+            pltpu.VMEM((5, chunks, parts, depth, width), F32),
             pltpu.VMEM((5, pd, ncase, nport), F32),
             pltpu.VMEM((5, nq, pd, ncase, nport), F32),
             pltpu.VMEM((5 * allcase, pd * nport), F32),
@@ -405,10 +455,10 @@
             pltpu.VMEM((parts, 8, allcase * allcase // 8), F32),
             pltpu.VMEM((modes, ncase * ncomp), F32),
             pltpu.VMEM((pd, ncase, nport), F32),
-            pltpu.SemaphoreType.DMA((9,)),
-            pltpu.SemaphoreType.DMA((9,)),
-            pltpu.SemaphoreType.DMA((5,)),
-            pltpu.SemaphoreType.DMA((5,)),
+            pltpu.SemaphoreType.DMA((3 + 5 * chunks,)),
+            pltpu.SemaphoreType.DMA((3 + 5 * chunks,)),
+            pltpu.SemaphoreType.DMA((5, nq)),
+            pltpu.SemaphoreType.DMA((5, nq)),
         ],
         compiler_params=pltpu.CompilerParams(
             collective_id=0, has_side_effects=True, vmem_limit_bytes=60 * 1024 * 1024

time: 80.3 us -> 76.9 us (0.958)
  Pallas kernels: 74.1 us -> 71.3 us
    pallas_call x1, Pallas kernels: 74.1 us -> 71.3 us  [local(): pl.pallas_call(body, out_shape=(jax.ShapeDtypeStruct(port_load.shape, F32...]
where the time goes in v2:
time: 76.9 us; the launch traced here: 76.7 us
  Pallas kernels  71.3 us (93%)
  local copies, waits for them, and re-layouts  4.05 us (5%)
    pallas_call x1, Pallas kernels, local(): pl.pallas_call(body, out_shape=(jax.ShapeDtypeStruct(port_load.shape, F32...  71.3 us
    unnamed x15, local copies, waits for them, and re-layouts  4.05 us

profile of v2, /device:TPU:0, one launch (start us, length us, event | category | flops | bytes accessed | tf_op | source)
XLA Modules:
  0.0 76.7 jit_solution(10221986592912961031)
XLA Ops:
  0.6 0.0 copy-start.5
  0.6 0.0 copy-start.2
  0.7 0.0 copy-start.3
  0.7 0.0 copy-start.4
  0.7 0.6 copy-done.5
  1.3 0.0 copy-done.2
  1.3 0.0 copy-done.3
  1.3 0.0 copy-done.4
  1.3 0.6 pad_add_fusion.refs_0_
  1.9 71.3 %condensed_solve.1 = (f32[48,8,128]{2,1,0:T(8,128)}, f32[48,8,128]{2,1,0:T(8,128)}, f32[64,8,128]{2,1,0:T(8,128)}) custom-call(s32[4,128]{1,0:T(4,128)} %pad_add_fusion.refs_0_, f32[1,128]{1,0:T(1,128)} %bitcast.7, f32[64,8,128]{2,1,0:T(8,128)} %refs_2_.1, f32[48,8,128]{2,1,0:T(8,128)} %refs_3_.1, f32[8,64,64]{2,1,0:T(8,128)} %refs_4_.1, ...), custom_call_target="tpu_custom_call" | custom-call | tf_op jit(solution)/shard_map/condensed_solve/pallas_call | solution.py:435
  73.3 0.0 copy-start.1
  73.3 1.7 %copy.16 = f32[48,8,128]{2,1,0:T(8,128)} copy(f32[48,8,128]{2,1,0:T(8,128)} %get-tuple-element.6) | data formatting | bytes 393216
  74.9 0.0 copy-done.1
  74.9 0.0 copy-start
  74.9 0.7 copy.17
  75.6 0.3 copy-done
  76.0 0.7 copy.18
Async XLA Ops:
  0.6 0.7 copy-start.5
  0.6 0.7 copy-start.2
  0.7 0.7 copy-start.3
  0.7 0.7 copy-start.4
  73.3 1.7 %copy-start.1 = (f32[48,8,128]{2,1,0:T(8,128)S(1)}, f32[48,8,128]{2,1,0:T(8,128)}, u32[]{:S(2)}) copy-start(f32[48,8,128]{2,1,0:T(8,128)} %get-tuple-element.7) | copy-start | bytes 589828
  74.9 1.0 %copy-start = (f32[64,8,128]{2,1,0:T(8,128)S(1)}, f32[64,8,128]{2,1,0:T(8,128)}, u32[]{:S(2)}) copy-start(f32[64,8,128]{2,1,0:T(8,128)} %get-tuple-element.8) | copy-start | bytes 786436

commit v3 on v2

--- a/solution.py
+++ b/solution.py
@@ -151,12 +151,8 @@
     rest = pl.ds(1, parts - 1)
     send_parts(lambda i: ask_send.at[i], lambda i: ask_recv.at[i], 0, 1)
 
-    red_t = [exact(binv_ref[t], coup_ref[t], TN) for t in range(kinds)]
-    schur = [pblock_ref[t] - exact(red_t[t], coup_ref[t], TN) for t in range(kinds)]
     inv_tab = split(jnp.concatenate([binv_ref[t] for t in range(kinds)], axis=1))
     coup_tab = split(jnp.concatenate([coup_ref[t].T for t in range(kinds)], axis=1))
-    schur_tab = split(jnp.concatenate(schur, axis=1))
-    red_tab = split(jnp.concatenate(red_t, axis=1))
 
     def tile_cases(row):
         return jnp.concatenate([row] * ncase, axis=1)
@@ -272,6 +268,10 @@
     leaving = tall(condensed[pd:])
     for j in range(chunks):
         start_far(0, j, slot_pick, part(leaving, j), 1)
+    red_t = [exact(binv_ref[t], coup_ref[t], TN) for t in range(kinds)]
+    schur = [pblock_ref[t] - exact(red_t[t], coup_ref[t], TN) for t in range(kinds)]
+    schur_tab = split(jnp.concatenate(schur, axis=1))
+    red_tab = split(jnp.concatenate(red_t, axis=1))
     own = jnp.concatenate([pload_ref[:, k, :] for k in range(ncase)], axis=0)
     own = own + pick(tall(condensed[:pd]), near_out)
     wait_on(ask_recv.at[rest], part_rsem.at[0])

time: 76.9 us -> 75.8 us (0.986)
  Pallas kernels: 71.3 us -> 70.3 us
    pallas_call x1, Pallas kernels: 71.3 us -> 70.3 us  [local(): pl.pallas_call(body, out_shape=(jax.ShapeDtypeStruct(port_load.shape, F32...]
where the time goes in v3:
time: 75.8 us; the launch traced here: 75.6 us
  Pallas kernels  70.3 us (93%)
  local copies, waits for them, and re-layouts  4.05 us (5%)
    pallas_call x1, Pallas kernels, local(): pl.pallas_call(body, out_shape=(jax.ShapeDtypeStruct(port_load.shape, F32...  70.3 us
    unnamed x15, local copies, waits for them, and re-layouts  4.05 us

profile of v3, /device:TPU:0, one launch (start us, length us, event | category | flops | bytes accessed | tf_op | source)
XLA Modules:
  0.0 75.6 jit_solution(17311632650527787299)
XLA Ops:
  0.6 0.0 copy-start.5
  0.6 0.0 copy-start.2
  0.7 0.0 copy-start.3
  0.7 0.0 copy-start.4
  0.7 0.6 copy-done.5
  1.3 0.0 copy-done.2
  1.3 0.0 copy-done.3
  1.3 0.0 copy-done.4
  1.3 0.6 pad_add_fusion.refs_0_
  1.9 70.3 %condensed_solve.1 = (f32[48,8,128]{2,1,0:T(8,128)}, f32[48,8,128]{2,1,0:T(8,128)}, f32[64,8,128]{2,1,0:T(8,128)}) custom-call(s32[4,128]{1,0:T(4,128)} %pad_add_fusion.refs_0_, f32[1,128]{1,0:T(1,128)} %bitcast.7, f32[64,8,128]{2,1,0:T(8,128)} %refs_2_.1, f32[48,8,128]{2,1,0:T(8,128)} %refs_3_.1, f32[8,64,64]{2,1,0:T(8,128)} %refs_4_.1, ...), custom_call_target="tpu_custom_call" | custom-call | tf_op jit(solution)/shard_map/condensed_solve/pallas_call | solution.py:435
  72.2 0.0 copy-start.1
  72.2 1.7 %copy.16 = f32[48,8,128]{2,1,0:T(8,128)} copy(f32[48,8,128]{2,1,0:T(8,128)} %get-tuple-element.6) | data formatting | bytes 393216
  73.9 0.0 copy-done.1
  73.9 0.0 copy-start
  73.9 0.7 copy.17
  74.5 0.3 copy-done
  74.9 0.7 copy.18
Async XLA Ops:
  0.6 0.7 copy-start.5
  0.6 0.7 copy-start.2
  0.7 0.7 copy-start.3
  0.7 0.7 copy-start.4
  72.2 1.7 %copy-start.1 = (f32[48,8,128]{2,1,0:T(8,128)S(1)}, f32[48,8,128]{2,1,0:T(8,128)}, u32[]{:S(2)}) copy-start(f32[48,8,128]{2,1,0:T(8,128)} %get-tuple-element.7) | copy-start | bytes 589828
  73.9 1.0 %copy-start = (f32[64,8,128]{2,1,0:T(8,128)S(1)}, f32[64,8,128]{2,1,0:T(8,128)}, u32[]{:S(2)}) copy-start(f32[64,8,128]{2,1,0:T(8,128)} %get-tuple-element.8) | copy-start | bytes 786436
